TPU v7x, 32 devices: a whole 2x2x4 slice. The times are simulated.
32 devices in a mesh: seq: 32 (over z, y, x, core), head: 1.
Axes of the slice: x: 2, y: 2, z: 4, core: 2. Of those that a mesh axis runs over, the one named last changes fastest.
Arguments:
- queries: bfloat16 [8192, 2048], P('seq', 'head'), may hold values from -6 to 6
- key_vectors: bfloat16 [8192, 2048], P('seq', 'head'), may hold values from -6 to 6
- value_vectors: bfloat16 [8192, 2048], P('seq', 'head'), may hold values from -6 to 6
- forget_gates: float32 [8192, 16], P('seq', 'head'), may hold values from 0.4 to 1, as said below
- shard_counts: int32 [32], P('seq'), may hold values from 1 to 256, 6144 in all
- gram_start: float32 [16, 128, 128], P('head'), may hold values from -4 to 12, as said below
- memory_start: float32 [16, 128, 128], P('head'), may hold values from -6 to 6
- ridge_terms: float32 [16, 128], P('head'), may hold values from 0.05 to 1
- norm_gain: float32 [2048], P('head'), may hold values from 0.1 to 1.9
- out_weight: bfloat16 [2048, 2048], P('head'), may hold values from -0.125 to 0.125
Outputs:
- mixed_out: bfloat16 [8192, 2048], P('seq', 'head')
Inputs may be any that keep to these rules, and one draw needn't show every extreme that they name: `shard_counts`: slots of a shard at local positions from its count on are padding; at least one shard is full. `forget_gates`: each gate lies in (0, 1]. `gram_start`: each head's matrix is symmetric positive semidefinite.
All inputs are finite; a program needn't handle non-finite values.
Results may differ from a plain program's by a relative error of at most 0.02.
Values may be sent and summed in bfloat16 or wider, within the bound.
No kernel may reach another device: no remote copies, remote signals or barrier semaphores. Data moves between devices by JAX's collectives and lax.ppermute only.
A program may use at most 128 MiB of HBM per device.

v0:
```python
import jax
import jax.numpy as jnp
from jax import lax
from jax.sharding import PartitionSpec as P

ITERS = 16


precise = lax.Precision.HIGHEST


def prefix(shard, axis, join, neutral):
    place = lax.axis_index(axis)
    gathered = jax.tree.map(
        lambda a, kind: lax.all_gather(a.astype(kind), axis),
        shard,
        (jnp.bfloat16, jnp.bfloat16, jnp.bfloat16),
    )
    state = jax.tree.map(lambda a, e: jnp.zeros_like(a) + jnp.asarray(e, a.dtype), shard, neutral)

    def one(turn, state):
        return join(
            state,
            jax.tree.map(
                lambda a, own: lax.dynamic_index_in_dim(a, turn, 0, False).astype(own.dtype),
                gathered,
                shard,
            ),
        )

    return lax.fori_loop(0, place, one, state)


def unit_rows(matrix):
    return matrix * lax.rsqrt(jnp.sum(matrix * matrix, axis=-1, keepdims=True) + 1e-06)


def summarize(key_rows, value_rows, running):
    tail_decay = jnp.exp(running[:, -1:] - running)[..., None]
    weighted = key_rows * tail_decay
    gram_local = jnp.einsum("hcd,hce->hde", weighted, key_rows, precision=precise)
    memory_local = jnp.einsum("hce,hcd->hed", value_rows, weighted, precision=precise)
    return (jnp.exp(running[:, -1]), gram_local, memory_local)


def solve_block(query_rows, key_rows, value_rows, running, gram_prev, memory_prev, ridge_terms):
    span_rows = running.shape[1]
    log_gaps = running[:, :, None] - running[:, None, :]
    lower_mask = lax.iota(jnp.int32, span_rows)[:, None] >= lax.iota(jnp.int32, span_rows)[None, :]
    within_block = jnp.where(lower_mask[None], jnp.exp(jnp.minimum(log_gaps, 0.0)), 0.0)
    lead_decay = jnp.exp(running)[..., None]
    ridge_diag = ridge_terms[:, None, :]

    def apply_op(vector_in, state_mat, rows_in):
        near_terms = (
            jnp.einsum("hcd,hsd->hcs", vector_in, key_rows, precision=precise) * within_block
        )
        return lead_decay * jnp.einsum(
            "hcd,hed->hce", vector_in, state_mat, precision=precise
        ) + jnp.einsum("hcs,hse->hce", near_terms, rows_in, precision=precise)

    def cg_step(loop_index, state_tuple):
        answer, residual, direction, norm_now = state_tuple
        image_vec = apply_op(direction, gram_prev, key_rows) + ridge_diag * direction
        step_size = norm_now / jnp.sum(direction * image_vec, axis=-1, keepdims=True)
        answer = answer + step_size * direction
        residual = residual - step_size * image_vec
        norm_next = jnp.sum(residual * residual, axis=-1, keepdims=True)
        direction = residual + norm_next / norm_now * direction
        return (answer, residual, direction, norm_next)

    initial = (
        jnp.zeros_like(query_rows),
        query_rows,
        query_rows,
        jnp.sum(query_rows * query_rows, axis=-1, keepdims=True),
    )
    answer = lax.fori_loop(0, ITERS, cg_step, initial)[0]
    return apply_op(answer, memory_prev, value_rows)


def combine(earlier, latter):
    scale_now = latter[0][..., None, None]
    return (
        earlier[0] * latter[0],
        scale_now * earlier[1] + latter[1],
        scale_now * earlier[2] + latter[2],
    )


def local(
    queries,
    key_vectors,
    value_vectors,
    forget_gates,
    shard_counts,
    gram_start,
    memory_start,
    ridge_terms,
    norm_gain,
    out_weight,
):
    row_count = queries.shape[0]
    heads_here = forget_gates.shape[1]
    head_width = queries.shape[1] // heads_here
    is_live = (lax.iota(jnp.int32, row_count) < shard_counts[0]).astype(jnp.float32)[:, None]

    def split_heads(matrix):
        return jnp.transpose(
            matrix.astype(jnp.float32).reshape(row_count, heads_here, head_width), (1, 0, 2)
        )

    query_rows = unit_rows(split_heads(queries))
    key_rows = unit_rows(split_heads(key_vectors)) * is_live[None]
    value_rows = split_heads(value_vectors) * is_live[None]
    log_decay = jnp.transpose(jnp.where(is_live > 0, jnp.log(forget_gates), 0.0))
    running = jnp.cumsum(log_decay, axis=1)
    decay_total, gram_local, memory_local = summarize(key_rows, value_rows, running)
    identity = (
        jnp.ones_like(decay_total),
        jnp.zeros_like(gram_local),
        jnp.zeros_like(memory_local),
    )
    before = prefix((decay_total, gram_local, memory_local), "seq", combine, identity)
    gram_prev = before[0][:, None, None] * gram_start + before[1]
    memory_prev = before[0][:, None, None] * memory_start + before[2]
    output = solve_block(
        query_rows, key_rows, value_rows, running, gram_prev, memory_prev, ridge_terms
    )
    scaled = output * lax.rsqrt(jnp.mean(output * output, axis=-1, keepdims=True) + 1e-05)
    flat_rows = (
        jnp.transpose(scaled, (1, 0, 2)).reshape(row_count, heads_here * head_width)
        * norm_gain[None, :]
        * is_live
    )
    normalized = flat_rows.astype(jnp.bfloat16)
    partial_terms = jnp.dot(normalized, out_weight, preferred_element_type=jnp.float32)
    return lax.psum_scatter(
        partial_terms.astype(jnp.bfloat16), "head", scatter_dimension=1, tiled=True
    )


def solution(mesh):
    return jax.shard_map(
        local,
        mesh=mesh,
        in_specs=(
            P("seq", "head"),
            P("seq", "head"),
            P("seq", "head"),
            P("seq", "head"),
            P("seq"),
            P("head", None, None),
            P("head", None, None),
            P("head", None),
            P("head"),
            P("head", None),
        ),
        out_specs=P("seq", "head"),
        check_vma=False,
    )
```

profile of v0, /device:TPU:31, one launch (start us, length us, event | category | flops | bytes accessed | tf_op | source)
XLA Modules:
  0.0 719.8 jit_solution(9566088236001363722)
XLA Ops:
  21.4 40.0 %all-reduce = bf16[512]{0:T(512)(128)(2,1)S(1)} all-reduce(bf16[512]{0:T(512)(128)(2,1)S(1)} %dynamic-update-slice), channel_id=2, replica_groups=mesh['seq'=32,'head'=1] {'seq'}, use_global_device_ids=true, to_apply=%add | all-reduce | flops 512 | bytes 2048
  65.4 66.4 %all-gather.8.cloned.1.call-done = bf16[512,128,128]{2,1,0:T(8,128)(2,1)} async-done(((bf16[16,128,128]{2,1,0:T(8,128)(2,1)}), bf16[512,128,128]{2,1,0:T(8,128)(2,1)}) %all-gather.8.cloned.1.call-update) | async-done | bytes 16777232 | tf_op jit(solution)/shard_map/all_gather | solution.py:15
  131.8 115.4 %all-gather.6.cloned.1.call-done = bf16[512,128,128]{2,1,0:T(8,128)(2,1)} async-done(((bf16[16,128,128]{2,1,0:T(8,128)(2,1)}), bf16[512,128,128]{2,1,0:T(8,128)(2,1)}) %all-gather.6.cloned.1.call-update) | async-done | bytes 16777232 | tf_op jit(solution)/shard_map/all_gather | solution.py:15
  248.4 94.2 %while.31 = (s32[]{:T(128)}, f32[16]{0:T(128)S(1)}, f32[16,128,128]{2,1,0:T(8,128)S(1)}, f32[16,128,128]{2,1,0:T(8,128)}, s32[]{:T(128)}, /*index=5*/bf16[32,16]...) while((s32[]{:T(128)}, f32[16]{0:T(128)S(1)}, ...), condition=%wide.region_6.7_spmd, body=%wide.region_5.6_spmd.sunk | while | flops 1572901 | bytes 5243319 | solution.py:31
  345.1 349.3 %while.32 = (s32[]{:T(128)}, f32[16,256,128]{1,2,0:T(8,128)}, f32[16,256,128]{1,2,0:T(8,128)}, f32[16,256,128]{1,2,0:T(8,128)S(1)}, f32[16,256,1]{1,0,2:T(8,128)...) while((s32[]{:T(128)}, f32[16,256,128]{1,2,0:T(8,128)}, ...), condition=%wide.region_10.11_spmd.clone, body=%wide.region_7.10_spmd.clone.sunk | while | flops 4038590464 | bytes 53797052 | solution.py:78
  345.1 5.7 fusion.84
  350.8 5.5 fusion.85
  358.9 3.3 multiply_reduce_fusion.9
  362.2 4.1 multiply_add_fusion.4
  366.3 5.7 fusion.84
  372.0 5.5 fusion.85
  380.1 3.3 multiply_reduce_fusion.9
  383.4 4.8 multiply_add_fusion.4
  388.2 5.7 fusion.84
  393.9 5.5 fusion.85
  402.0 3.3 multiply_reduce_fusion.9
  405.3 4.8 multiply_add_fusion.4
  410.0 5.7 fusion.84
  415.8 5.5 fusion.85
  423.8 3.3 multiply_reduce_fusion.9
  427.1 4.8 multiply_add_fusion.4
  431.9 5.7 fusion.84
  437.6 5.5 fusion.85
  445.7 3.3 multiply_reduce_fusion.9
  449.0 4.8 multiply_add_fusion.4
  453.8 5.7 fusion.84
  459.5 5.5 fusion.85
  467.6 3.3 multiply_reduce_fusion.9
  470.9 4.8 multiply_add_fusion.4
  475.6 5.7 fusion.84
  481.4 5.5 fusion.85
  492.8 4.8 multiply_add_fusion.4
  497.5 5.7 fusion.84
  503.2 5.5 fusion.85
  511.3 3.3 multiply_reduce_fusion.9
  514.6 4.8 multiply_add_fusion.4
  519.4 5.7 fusion.84
  525.1 5.5 fusion.85
  533.2 3.3 multiply_reduce_fusion.9
  536.5 4.8 multiply_add_fusion.4
  541.3 5.7 fusion.84
  547.0 5.5 fusion.85
  558.4 4.8 multiply_add_fusion.4
  563.1 5.7 fusion.84
  568.9 5.5 fusion.85
  580.2 4.8 multiply_add_fusion.4
  585.0 5.7 fusion.84
  590.7 5.5 fusion.85
  602.1 4.8 multiply_add_fusion.4
  606.9 5.7 fusion.84
  612.6 5.5 fusion.85
  624.0 4.8 multiply_add_fusion.4
  628.7 5.7 fusion.84
  634.5 5.5 fusion.85
  645.8 4.8 multiply_add_fusion.4
  650.6 5.7 fusion.84
  656.3 5.5 fusion.85
  667.7 4.8 multiply_add_fusion.4
  672.5 5.7 fusion.84
  678.2 5.5 fusion.85
  689.6 4.8 multiply_add_fusion.4
  694.4 6.3 fusion.57
  702.9 5.6 multiply_reduce_fusion.2
  709.6 3.3 convolution_convert_fusion
  (267 shorter events, 186.5 us)
Async XLA Ops:
  6.5 125.3 %all-gather.8.cloned.1.call-start = ((), (), s32[]{:S(2)}) async-start(), calls=%async_computation.1 | async-start | bytes 17301504 | tf_op jit(solution)/shard_map/all_gather | solution.py:15
  9.1 1.8 copy-start.8
  10.7 2.0 copy-start.5
  12.6 2.2 copy-start.6
  14.7 3.3 copy-start
  17.9 43.6 %copy-start.9 = (bf16[256,2048]{1,0:T(8,128)(2,1)S(1)}, bf16[256,2048]{1,0:T(8,128)(2,1)}, u32[]{:S(2)}) copy-start(bf16[256,2048]{1,0:T(8,128)(2,1)} %param.14) | copy-start | bytes 3145732
  17.9 229.3 %all-gather.6.cloned.1.call-start = ((), (), s32[]{:S(2)}) async-start(), calls=%async_computation | async-start | bytes 17301504 | tf_op jit(solution)/shard_map/all_gather | solution.py:15
  342.7 2.4 copy-start.11
  345.1 5.7 copy-start.1
  350.8 5.5 copy-start.4
  366.3 5.7 copy-start.1
  372.0 5.5 copy-start.4
  388.2 5.7 copy-start.1
  393.9 5.5 copy-start.4
  410.0 5.7 copy-start.1
  415.8 5.5 copy-start.4
  431.9 5.7 copy-start.1
  437.6 5.5 copy-start.4
  453.8 5.7 copy-start.1
  459.5 5.5 copy-start.4
  475.6 5.7 copy-start.1
  481.4 5.5 copy-start.4
  497.5 5.7 copy-start.1
  503.2 5.5 copy-start.4
  519.4 5.7 copy-start.1
  525.1 5.5 copy-start.4
  541.2 5.7 copy-start.1
  547.0 5.5 copy-start.4
  563.1 5.7 copy-start.1
  568.8 5.5 copy-start.4
  585.0 5.7 copy-start.1
  590.7 5.5 copy-start.4
  606.9 5.7 copy-start.1
  612.6 5.5 copy-start.4
  628.7 5.7 copy-start.1
  634.5 5.5 copy-start.4
  650.6 5.7 copy-start.1
  656.3 5.5 copy-start.4
  672.5 5.7 copy-start.1
  678.2 5.5 copy-start.4
  694.3 6.3 copy-start.2
  694.3 6.3 copy-start.3
  694.3 6.4 copy-start.10
  700.7 2.2 copy-start.7
  700.7 8.8 %slice-start = ((s8[8388608]{0:T(1024)(128)(4,1)}), s8[4194304]{0:T(1024)(128)(4,1)S(1)}, s32[]{:S(2)}) async-start(s8[8388608]{0:T(1024)(128)(4,1)} %bitcast.123), calls=%async_computation.2 | async-start | bytes 8388608
  702.9 6.7 slice-start.1
  708.5 0.7 copy-start.12
Sparse Core Ops, SparseCore 0:
  18.0 113.7 all-gather.7
  134.6 112.5 all-gather.5
where the time goes:
time: 722 us; the launch traced here: 720 us
  matrix products  243 us (34%)
  other arithmetic  232 us (32%)
  waiting for transfers between devices  182 us (25%)
  blocking collectives  40 us (6%)
  between operations  14.4 us (2%)
  local copies, waits for them, and re-layouts  8.07 us (1%)
    all_gather x2, waiting for transfers between devices, prefix(): lax.all_gather(a.astype(kind), axis)  182 us
    dot_general x17, matrix products, apply_op(): jnp.einsum('hcd,hsd->hcs', vector_in, key_rows, precision=precise)  97.6 us
    add x31, other arithmetic, combine(): scale_now * earlier[2] + latter[2]  93.8 us
    dot_general x17, matrix products, apply_op(): jnp.einsum('hcs,hse->hce', near_terms, rows_in, precision=precise)  93.3 us
    add x16, other arithmetic, cg_step(): direction = residual + norm_next / norm_now * direction  75.5 us
    reduce_sum x16, other arithmetic, cg_step(): norm_next = jnp.sum(residual * residual, axis=-1, keepdims=True)  52.9 us
    dot_general x17, matrix products, apply_op(): jnp.einsum('hcd,hed->hce', vector_in, state_mat, precision=precise)  42.8 us
    unnamed x1, blocking collectives  40 us
  transfers between devices with their start and end apart: 2, of which 2 were waited for; matrix products, arithmetic and copies ran while one was open for 1% of the time, Pallas kernels for 0%

commit v1 on v0

v1 whole, which is shorter than its diff:
```python
import functools

import jax
import jax.numpy as jnp
from jax import lax
from jax.experimental import pallas as pl
from jax.experimental.pallas import tpu as pltpu
from jax.sharding import PartitionSpec as P

ITERS = 16
FINE = 9
F = jnp.float32
B = jnp.bfloat16
DEAD = 1e30
VMEM_BYTES = 56 << 20


def split(a):
    hi = a.astype(B)
    return hi, (a - hi.astype(F)).astype(B)


def dot(a, b):
    return jnp.dot(a, b, preferred_element_type=F)


def spec(block, index):
    return pl.BlockSpec(block, index)


def whole(shape):
    zeros = (0,) * len(shape)
    return pl.BlockSpec(shape, lambda *_: zeros)


SMEM = pl.BlockSpec(memory_space=pltpu.SMEM)


def params():
    return pltpu.CompilerParams(vmem_limit_bytes=VMEM_BYTES)


def gates_kernel(count, gates, run_out, wide):
    tokens, heads = gates.shape
    at = lax.broadcasted_iota(jnp.int32, (tokens, heads), 0)
    logs = jnp.where(at < count[0], jnp.log(gates[...]), 0.0)
    wide[...] = jnp.zeros_like(wide)
    wide[:, :heads] = logs
    row = lax.broadcasted_iota(jnp.int32, (tokens, tokens), 0)
    col = lax.broadcasted_iota(jnp.int32, (tokens, tokens), 1)
    upper = (row <= col).astype(F)
    run_out[...] = jnp.dot(
        wide[...].T[:heads], upper, preferred_element_type=F, precision=lax.Precision.HIGHEST
    )


def gates_call(count, gates):
    tokens, heads = gates.shape
    return pl.pallas_call(
        gates_kernel,
        in_specs=[SMEM, whole(gates.shape)],
        out_specs=whole((heads, tokens)),
        out_shape=jax.ShapeDtypeStruct((heads, tokens), F),
        scratch_shapes=[pltpu.VMEM((tokens, 128), F)],
        name="gates",
    )(count, gates)


def sums_kernel(chunk, width, gram, count, keys, others, run, sums_out, pay_out, keyt_out, norm_out):
    tokens = keys.shape[0]
    at = lax.broadcasted_iota(jnp.int32, (1, tokens), 1)
    live = (at < count[0]).astype(F)
    for j in range(chunk):
        cols = slice(j * width, (j + 1) * width)
        key = keys[:, cols]
        keyt = key.astype(F).T
        square = jnp.sum(keyt * keyt, axis=0, keepdims=True) + 1e-06
        now = run[j : j + 1, :]
        last = now[:, tokens - 1 :]
        tail = jnp.exp(last - now) * live
        if gram:
            left = keyt * (tail / square)
            keyt_out[j] = keyt.astype(B)
            norm_out[j : j + 1, :] = square
        else:
            left = others[:, cols].astype(F).T * (tail * lax.rsqrt(square))
        hi, lo = split(left)
        both = dot(jnp.concatenate([hi, lo], 1), jnp.concatenate([key, key], 0))
        sums_out[j, :width] = both
        pay_out[j, :width] = both.astype(B)
        decay = jnp.broadcast_to(jnp.exp(last), (1, width))
        first = decay.astype(B)
        second, third = split(decay - first.astype(F))
        sums_out[j, width:] = jnp.broadcast_to(decay, (8, width))
        row = lax.broadcasted_iota(jnp.int32, (16, width), 0)
        pay_out[j, width:] = jnp.where(
            row == 0,
            first.astype(F),
            jnp.where(row == 1, second.astype(F), jnp.where(row == 2, third.astype(F), 0.0)),
        ).astype(B)


def sums_call(count, keys, others, run, chunk, place, gram):
    tokens = keys.shape[0]
    heads = run.shape[0]
    width = keys.shape[1] // heads
    block = spec((tokens, chunk * width), lambda i: (0, place))
    shapes = [
        jax.ShapeDtypeStruct((chunk, width + 8, width), F),
        jax.ShapeDtypeStruct((chunk, width + 16, width), B),
    ]
    if gram:
        shapes += [
            jax.ShapeDtypeStruct((chunk, width, tokens), B),
            jax.ShapeDtypeStruct((chunk, tokens), F),
        ]

    def body(count_ref, keys_ref, *rest):
        if gram:
            run_ref, *outs = rest
            sums_kernel(chunk, width, True, count_ref, keys_ref, None, run_ref, *outs)
        else:
            others_ref, run_ref, *outs = rest
            sums_kernel(chunk, width, False, count_ref, keys_ref, others_ref, run_ref, *outs, None, None)

    mine = run.reshape(heads // chunk, chunk, tokens)[place]
    ins = [count, keys] + ([] if gram else [others]) + [mine]
    return pl.pallas_call(
        body,
        grid=(1,),
        in_specs=[SMEM, block] + ([] if gram else [block]) + [whole(mine.shape)],
        out_specs=[whole(s.shape) for s in shapes],
        out_shape=shapes,
        compiler_params=params(),
        name="gram_sums" if gram else "memory_sums",
    )(*ins)


def decay_of(pay, j, width):
    rows = pay[j, width:].astype(F)
    return rows[0:1] + rows[1:2] + rows[2:3]


def put(pay_out, j, width, total, decay):
    pay_out[j, :width] = total.astype(B)
    first = decay.astype(B)
    second, third = split(decay - first.astype(F))
    row = lax.broadcasted_iota(jnp.int32, (16, width), 0)
    pay_out[j, width:] = jnp.where(
        row == 0,
        first.astype(F),
        jnp.where(row == 1, second.astype(F), jnp.where(row == 2, third.astype(F), 0.0)),
    ).astype(B)


def pair_kernel(half, width, side, own, got, total_out, pay_out):
    c = side[0]
    for j in range(half):
        at = c * half + j
        mine, decay = own[at, :width], own[at, width : width + 1]
        other, other_decay = got[at, :width].astype(F), decay_of(got, at, width)
        total = jnp.where(c == 0, other_decay, 1.0) * mine + jnp.where(c == 0, 1.0, decay) * other
        both = decay * other_decay
        total_out[j, :width] = total
        total_out[j, width:] = jnp.broadcast_to(both, (8, width))
        put(pay_out, j, width, total, both)


def pair_call(side, own, got, half):
    width = own.shape[2]
    shapes = [
        jax.ShapeDtypeStruct((half, width + 8, width), F),
        jax.ShapeDtypeStruct((half, width + 16, width), B),
    ]
    return pl.pallas_call(
        functools.partial(pair_kernel, half, width),
        in_specs=[SMEM, whole(own.shape), whole(got.shape)],
        out_specs=[whole(s.shape) for s in shapes],
        out_shape=shapes,
        compiler_params=params(),
        name="pair",
    )(side, own, got)


def group_kernel(radix, half, width, first, side, own, *rest):
    gots = rest[: radix - 1]
    rest = rest[radix - 1 :]
    if first:
        before = None
        total_out, pay_out, before_out = rest
    else:
        before, total_out, pay_out, before_out = rest
    p = side[0]
    for j in range(half):
        terms = [own[j, :width]] + [g[j, :width].astype(F) for g in gots]
        decays = [own[j, width : width + 1]] + [decay_of(g, j, width) for g in gots]
        total = jnp.zeros_like(terms[0])
        prefix = jnp.zeros_like(terms[0])
        prefix_decay = jnp.ones_like(decays[0])
        for m in range(radix):
            k = p ^ m
            coef = jnp.ones_like(decays[0])
            lead = jnp.ones_like(decays[0])
            for n in range(radix):
                if n != m:
                    o = p ^ n
                    coef = coef * jnp.where(o > k, decays[n], 1.0)
                    if n != 0:
                        lead = lead * jnp.where((o > k) & (o < p), decays[n], 1.0)
            total = total + coef * terms[m]
            if m != 0:
                prefix = prefix + jnp.where(k < p, lead, 0.0) * terms[m]
                prefix_decay = prefix_decay * jnp.where(k < p, decays[m], 1.0)
        every = decays[0]
        for n in range(1, radix):
            every = every * decays[n]
        if not first:
            inner = before[j, width : width + 1]
            prefix = inner * prefix + before[j, :width]
            prefix_decay = inner * prefix_decay
        total_out[j, :width] = total
        total_out[j, width:] = jnp.broadcast_to(every, (8, width))
        put(pay_out, j, width, total, every)
        before_out[j, :width] = prefix
        before_out[j, width:] = jnp.broadcast_to(prefix_decay, (8, width))


def group_call(side, own, gots, before):
    half, _, width = own.shape
    shapes = [
        jax.ShapeDtypeStruct((half, width + 8, width), F),
        jax.ShapeDtypeStruct((half, width + 16, width), B),
        jax.ShapeDtypeStruct((half, width + 8, width), F),
    ]
    ins = [side, own, *gots] + ([] if before is None else [before])
    return pl.pallas_call(
        functools.partial(group_kernel, len(gots) + 1, half, width, before is None),
        in_specs=[SMEM] + [whole(a.shape) for a in ins[1:]],
        out_specs=[whole(s.shape) for s in shapes],
        out_shape=shapes,
        compiler_params=params(),
        name="group",
    )(*ins)


def last_kernel(radix, half, width, first, side, start, *rest):
    gots = rest[: radix - 1]
    before = None if first else rest[radix - 1]
    out = rest[-1]
    p = side[1]
    base = side[0] * half
    for j in range(half):
        prefix = jnp.zeros((width, width), F)
        gone = jnp.ones((1, width), F)
        for m, g in enumerate(gots, 1):
            prefix = prefix + gone * g[j, :width].astype(F)
            gone = gone * jnp.where(p >= m, decay_of(g, j, width), 1.0)
        total = gone * start[base + j] + prefix
        if not first:
            total = before[j, width : width + 1] * total + before[j, :width]
        out[j] = total


def last_call(side, start, gots, before, chunk, place):
    half, _, width = gots[0].shape
    ins = [side, start, *gots] + ([] if before is None else [before])
    block = spec((chunk, width, width), lambda i: (place, 0, 0))
    return pl.pallas_call(
        functools.partial(last_kernel, len(gots) + 1, half, width, before is None),
        grid=(1,),
        in_specs=[SMEM, block] + [whole(a.shape) for a in ins[2:]],
        out_specs=whole((half, width, width)),
        out_shape=jax.ShapeDtypeStruct((half, width, width), F),
        compiler_params=params(),
        name="last",
    )(*ins)


def radices(count):
    rest = count // 2
    out = []
    while rest > 1:
        step = 4 if rest % 4 == 0 else 2
        out.append(step)
        rest //= step
    return out


def prefix(sums, pay, start, count, chunk, place):
    me = lax.axis_index("seq").astype(jnp.int32)
    half = chunk // 2

    def send(a, moves):
        return lax.ppermute(a, "seq", moves)

    got = send(pay, [(i, i ^ 1) for i in range(count)])
    first = got
    side = jnp.stack([me & 1])
    total, pay = pair_call(side, sums, got, half)
    before = None
    stride = 2
    steps = radices(count)
    for n, radix in enumerate(steps):
        spot = (me // stride) % radix
        if n < len(steps) - 1:
            gots = [
                send(pay, [(i, i ^ (m * stride)) for i in range(count)]) for m in range(1, radix)
            ]
            total, pay, before = group_call(jnp.stack([spot]), total, gots, before)
        else:
            gots = [
                send(pay, [(i, i + m * stride) for i in range(count - m * stride)])
                for m in range(1, radix)
            ]
            mine = last_call(jnp.stack([me & 1, spot]), start, gots, before, chunk, place)
        stride *= radix
    theirs = send(mine, [(i, i ^ 1) for i in range(count)])
    return mine, theirs, first


def state_of(c, j, half, width, mine, theirs, first):
    at = j % half
    same = c == j // half
    before = jnp.where(same, mine[at], theirs[at])
    decay = jnp.where(c == 0, 1.0, decay_of(first, j, width))
    local = jnp.where(c == 0, 0.0, first[j, :width].astype(F))
    return decay * before + local


def weights_kernel(chunk, width, count, queries, run, norm, weight_out, query_out, wide):
    tokens = queries.shape[0]
    at = lax.broadcasted_iota(jnp.int32, (1, tokens), 1)
    now = run[...]
    wide[...] = jnp.zeros_like(wide)
    wide[:chunk] = jnp.where(at < count[0], now + jnp.log(norm[...]), DEAD)
    tall = wide[...].T
    row = lax.broadcasted_iota(jnp.int32, (tokens, tokens), 0)
    col = lax.broadcasted_iota(jnp.int32, (tokens, tokens), 1)
    for j in range(chunk):
        weight_out[j] = jnp.where(row <= col, jnp.exp(now[j : j + 1] - tall[:, j : j + 1]), 0.0)
        q = queries[:, j * width : (j + 1) * width].astype(F).T
        query_out[j] = q * lax.rsqrt(jnp.sum(q * q, axis=0, keepdims=True) + 1e-06)


def weights_call(count, queries, run, norm, chunk, place):
    tokens = queries.shape[0]
    heads = run.shape[0]
    width = queries.shape[1] // heads
    mine = run.reshape(heads // chunk, chunk, tokens)[place]
    shapes = [
        jax.ShapeDtypeStruct((chunk, tokens, tokens), F),
        jax.ShapeDtypeStruct((chunk, width, tokens), F),
    ]
    return pl.pallas_call(
        functools.partial(weights_kernel, chunk, width),
        grid=(1,),
        in_specs=[
            SMEM,
            spec((tokens, chunk * width), lambda i: (0, place)),
            whole(mine.shape),
            whole(norm.shape),
        ],
        out_specs=[whole(s.shape) for s in shapes],
        out_shape=shapes,
        scratch_shapes=[pltpu.VMEM((128, tokens), F)],
        compiler_params=params(),
        name="weights",
    )(count, queries, mine, norm)


def solve_kernel(
    chunk, width, side, keys, keyt, queries, weights, run, ridge, mine, theirs, first,
    answer_out, left, dirs, resid, near_top, near_low, far,
):
    tokens = keys.shape[0]
    half_t = tokens // 2
    c = side[0]
    lead = []
    norms = []
    for j in range(chunk):
        key = keys[:, j * width : (j + 1) * width]
        left[j, :tokens, :width] = key
        left[j, :tokens, width:] = key
        gram = state_of(c, j, chunk // 2, width, mine, theirs, first).astype(B)
        left[j, tokens:, :width] = gram
        left[j, tokens:, width:] = gram
        q = queries[j]
        dirs[j] = q
        resid[j] = q
        answer_out[j] = jnp.zeros_like(q)
        norms.append(jnp.sum(q * q, axis=0, keepdims=True))
        lead.append(jnp.exp(run[j : j + 1, :]))

    def spread(j, fine):
        p = dirs[j]
        if fine:
            hi, lo = split(p)
            image = dot(left[j], jnp.concatenate([hi, lo], 0))
        else:
            image = dot(left[j, :, :width], p.astype(B))
        far[j] = image[tokens:]
        top = image[:half_t] * weights[j, :half_t]
        low = image[half_t:tokens, half_t:] * weights[j, half_t:, half_t:]
        if fine:
            near_top[j, 0], near_top[j, 1] = split(top)
            near_low[j, 0], near_low[j, 1] = split(low)
        else:
            near_top[j, 0] = top.astype(B)
            near_low[j, 0] = low.astype(B)

    def gather(j, fine, norm):
        kt = keyt[j]
        p = dirs[j]
        if fine:
            early = kt[:, :half_t]
            one = dot(
                jnp.concatenate([early, early], 1),
                jnp.concatenate([near_top[j, 0, :, :half_t], near_top[j, 1, :, :half_t]], 0),
            )
            two = dot(
                kt,
                jnp.concatenate(
                    [
                        jnp.concatenate([near_top[j, 0, :, half_t:], near_top[j, 1, :, half_t:]], 1),
                        jnp.concatenate([near_low[j, 0], near_low[j, 1]], 1),
                    ],
                    0,
                ),
            )
            near = jnp.concatenate([one, two[:, :half_t] + two[:, half_t:]], 1)
        else:
            low = near_low[j, 0]
            near = dot(
                kt,
                jnp.concatenate(
                    [near_top[j, 0], jnp.concatenate([jnp.zeros_like(low), low], 1)], 0
                ),
            )
        image = lead[j] * far[j] + near + ridge[j] * p
        step = norm / jnp.sum(p * image, axis=0, keepdims=True)
        answer_out[j] = answer_out[j] + step * p
        r = resid[j] - step * image
        resid[j] = r
        after = jnp.sum(r * r, axis=0, keepdims=True)
        dirs[j] = r + (after / norm) * p
        return after

    cut = max(chunk // 2, 1)
    pairs = list(zip(range(cut), range(cut, chunk)))

    def turn(fine, fine_next):
        def body(_, norms):
            norms = list(norms)
            for a, b in pairs:
                spread(b, fine)
                norms[a] = gather(a, fine, norms[a])
            for a, b in pairs:
                spread(a, fine_next)
                norms[b] = gather(b, fine, norms[b])
            return tuple(norms)

        return body

    for a, _ in pairs:
        spread(a, True)
    norms = lax.fori_loop(0, FINE - 1, turn(True, True), tuple(norms))
    norms = turn(True, False)(0, norms)
    lax.fori_loop(FINE, ITERS, turn(False, False), norms)


def solve_call(side, keys, keyt, queries, weights, run, ridge, state, chunk, place):
    tokens = keys.shape[0]
    heads = run.shape[0]
    width = keys.shape[1] // heads
    mine, theirs, first = state
    here = run.reshape(heads // chunk, chunk, tokens)[place]
    block = spec((tokens, chunk * width), lambda i: (0, place))
    ridge_block = spec((chunk, width, 1), lambda i: (place, 0, 0))
    ins = [side, keys, keyt, queries, weights, here, ridge[..., None], mine, theirs, first]
    return pl.pallas_call(
        functools.partial(solve_body, chunk, width),
        grid=(1,),
        in_specs=[SMEM, block]
        + [whole(a.shape) for a in ins[2:6]]
        + [ridge_block]
        + [whole(a.shape) for a in ins[7:]],
        out_specs=whole((chunk, width, tokens)),
        out_shape=jax.ShapeDtypeStruct((chunk, width, tokens), F),
        scratch_shapes=[
            pltpu.VMEM((chunk, tokens + width, 2 * width), B),
            pltpu.VMEM((chunk, width, tokens), F),
            pltpu.VMEM((chunk, width, tokens), F),
            pltpu.VMEM((chunk, 2, tokens // 2, tokens), B),
            pltpu.VMEM((chunk, 2, tokens // 2, tokens // 2), B),
            pltpu.VMEM((chunk, width, tokens), F),
        ],
        compiler_params=params(),
        name="solve",
    )(*ins)


def solve_body(chunk, width, side, keys, keyt, queries, weights, run, ridge, *rest):
    tokens = keys.shape[0]
    wide = [jnp.broadcast_to(ridge[j], (width, tokens)) for j in range(chunk)]
    solve_kernel(chunk, width, side, keys, keyt, queries, weights, run, wide, *rest)


def readout_kernel(
    chunk, width, pair, side, keys, values, answers, weights, run, norm, gain,
    mine, theirs, first, out_weight, count, into, out, total, state,
):
    tokens = keys.shape[0]
    i = pl.program_id(0)
    c = side[0]

    @pl.when(i == 0)
    def _():
        for j in range(chunk):
            state[j] = state_of(c, j, chunk // 2, width, mine, theirs, first).astype(B)
        total[...] = jnp.zeros_like(total) if into is None else into[...]

    at = lax.broadcasted_iota(jnp.int32, (1, tokens), 1)
    live = (at < count[0]).astype(F)
    rows = []
    for j in range(pair):
        cols = slice(j * width, (j + 1) * width)
        hi, lo = split(answers[j])
        both = jnp.concatenate([hi, lo], 0)
        key = keys[:, cols]
        near = (dot(jnp.concatenate([key, key], 1), both) * weights[j]).astype(B)
        value = (values[:, cols].astype(F).T * jnp.sqrt(norm[j])).astype(B)
        memory = state[i * pair + j]
        o = jnp.exp(run[j]) * dot(jnp.concatenate([memory, memory], 1), both) + dot(value, near)
        scale = lax.rsqrt(jnp.mean(o * o, axis=0, keepdims=True) + 1e-05) * live
        rows.append((o * scale).T * gain[:, cols])
    y = jnp.concatenate(rows, 1).astype(B)
    total[...] += dot(y, out_weight[...])

    @pl.when(i == pl.num_programs(0) - 1)
    def _():
        out[...] = total[...].astype(out.dtype)


def readout_call(
    side, keys, values, answers, weights, run, norm, gain, state, out_weight, count, into, chunk, place, last
):
    tokens = keys.shape[0]
    heads = run.shape[0]
    width = keys.shape[1] // heads
    model = out_weight.shape[1]
    pair = 2 if chunk % 2 == 0 else 1
    turns = chunk // pair
    base = place * turns
    here = run.reshape(heads // chunk, chunk, 1, tokens)[place]
    norm = norm.reshape(chunk, 1, tokens)
    mine, theirs, first = state
    tok = spec((tokens, pair * width), lambda i: (0, base + i))
    row = spec((pair, 1, tokens), lambda i: (i, 0, 0))
    ins = [side, keys, values, answers, weights, here, norm, gain.reshape(1, -1),
           mine, theirs, first, out_weight, count]
    in_specs = [
        SMEM,
        tok,
        tok,
        spec((pair, width, tokens), lambda i: (i, 0, 0)),
        spec((pair, tokens, tokens), lambda i: (i, 0, 0)),
        row,
        row,
        spec((1, pair * width), lambda i: (0, base + i)),
        whole(mine.shape),
        whole(theirs.shape),
        whole(first.shape),
        spec((pair * width, model), lambda i: (base + i, 0)),
        SMEM,
    ]
    if into is not None:
        ins.append(into)
        in_specs.append(whole(into.shape))

    def body(*refs):
        refs = list(refs)
        if into is None:
            refs.insert(13, None)
        readout_kernel(chunk, width, pair, *refs)

    return pl.pallas_call(
        body,
        grid=(turns,),
        in_specs=in_specs,
        out_specs=whole((tokens, model)),
        out_shape=jax.ShapeDtypeStruct((tokens, model), B if last else F),
        scratch_shapes=[
            pltpu.VMEM((tokens, model), F),
            pltpu.VMEM((chunk, width, width), B),
        ],
        compiler_params=params(),
        name="readout",
    )(*ins)


def local(
    shards, columns,
    queries, key_vectors, value_vectors, forget_gates, shard_counts, gram_start,
    memory_start, ridge_terms, norm_gain, out_weight,
):
    heads = forget_gates.shape[1]
    chunk = min(heads, 8)
    parts = range(heads // chunk)
    me = lax.axis_index("seq").astype(jnp.int32)
    side = jnp.stack([me & 1])
    run = gates_call(shard_counts, forget_gates)
    grams = [
        sums_call(shard_counts, key_vectors, None, run, chunk, n, True) for n in parts
    ]
    gram_states = [
        prefix(grams[n][0], grams[n][1], gram_start, shards, chunk, n) for n in parts
    ]
    memories = [
        sums_call(shard_counts, key_vectors, value_vectors, run, chunk, n, False) for n in parts
    ]
    memory_states = [
        prefix(memories[n][0], memories[n][1], memory_start, shards, chunk, n) for n in parts
    ]
    weights = [
        weights_call(shard_counts, queries, run, grams[n][3], chunk, n) for n in parts
    ]
    answers = [
        solve_call(
            side, key_vectors, grams[n][2], weights[n][1], weights[n][0], run, ridge_terms,
            gram_states[n], chunk, n,
        )
        for n in parts
    ]
    mixed = None
    for n in parts:
        mixed = readout_call(
            side, key_vectors, value_vectors, answers[n], weights[n][0], run, grams[n][3],
            norm_gain, memory_states[n], out_weight, shard_counts, mixed, chunk, n,
            n == len(parts) - 1,
        )
    if columns > 1:
        mixed = lax.psum_scatter(mixed, "head", scatter_dimension=1, tiled=True)
    return mixed


def solution(mesh):
    return jax.shard_map(
        functools.partial(local, mesh.shape["seq"], mesh.shape["head"]),
        mesh=mesh,
        in_specs=(
            P("seq", "head"),
            P("seq", "head"),
            P("seq", "head"),
            P("seq", "head"),
            P("seq"),
            P("head", None, None),
            P("head", None, None),
            P("head", None),
            P("head"),
            P("head", None),
        ),
        out_specs=P("seq", "head"),
        check_vma=False,
    )
```

time: 722 us -> 188 us (0.26)
  the two profiles are of different devices: /device:TPU:31 before, /device:TPU:0 now
where the time goes in v1:
time: 188 us; the launch traced here: 187 us
  Pallas kernels  107 us (57%)
  starting transfers between devices  61.7 us (33%)
  local copies, waits for them, and re-layouts  12.8 us (7%)
  waiting for transfers between devices  3.64 us (2%)
    ppermute x32, starting transfers between devices, send(): return lax.ppermute(a, 'seq', moves)  61.7 us
    pallas_call x2, Pallas kernels, solve_call(): pl.pallas_call(functools.partial(solve_body, chunk, width), grid=(1,), in...  45.1 us
    pallas_call x2, Pallas kernels, readout_call(): pl.pallas_call(body, grid=(turns,), in_specs=in_specs, out_specs=whole((t...  17 us
    pallas_call x4, Pallas kernels, sums_call(): pl.pallas_call(body, grid=(1,), in_specs=[SMEM, block] + ([] if gram else...  11.2 us
    pallas_call x4, Pallas kernels, group_call(): pl.pallas_call(functools.partial(group_kernel, len(gots) + 1, half, width...  8.65 us
    pallas_call x4, Pallas kernels, last_call(): pl.pallas_call(functools.partial(last_kernel, len(gots) + 1, half, width,...  8.52 us
    pallas_call x4, Pallas kernels, pair_call(): pl.pallas_call(functools.partial(pair_kernel, half, width), in_specs=[SME...  7.9 us
    unnamed x75, local copies, waits for them, and re-layouts  7.69 us
  transfers between devices with their start and end apart: 32, of which 2 were waited for; matrix products, arithmetic and copies ran while one was open for 2% of the time, Pallas kernels for 50%

profile of v1, /device:TPU:0, one launch (start us, length us, event | category | flops | bytes accessed | tf_op | source)
XLA Modules:
  0.0 186.9 jit_solution(7082447553357459632)
XLA Ops:
  0.7 1.5 copy.12.gates
  2.1 1.8 gates.2
  3.9 1.3 fusion
  5.2 2.8 %memory_sums.3 = (f32[8,136,128]{2,1,0:T(8,128)}, bf16[8,144,128]{2,1,0:T(8,128)(2,1)}) custom-call(s32[1]{0:T(128)S(6)} %copy.15.count.count_ref.refs_12_, bf16[256,2048]{1,0:T(8,128)(2,1)} %refs_1_.3, bf16[256,2048]{1,0:T(8,128)(2,1)} %refs_2_.3, f32[8,256]{1,0:T(8,128)} %get-tuple-element.69.rest_0_.run.rest_1_), custom_call_target="tpu_custom_call" | custom-call | tf_op jit(solution)/shard_map/memory_sums/pallas_call | solution.py:128
  8.5 2.8 %gram_sums.3 = (f32[8,136,128]{2,1,0:T(8,128)}, bf16[8,144,128]{2,1,0:T(8,128)(2,1)}, bf16[8,128,256]{2,1,0:T(8,128)(2,1)}, f32[8,256]{1,0:T(8,128)}) custom-call(s32[1]{0:T(128)S(6)} %copy.15.count.count_ref.refs_12_, bf16[256,2048]{1,0:T(8,128)(2,1)} %refs_1_.3, f32[8,256]{1,0:T(8,128)} %get-tuple-element.69.rest_0_.run.rest_1_), custom_call_target="tpu_custom_call" | custom-call | tf_op jit(solution)/shard_map/gram_sums/pallas_call | solution.py:128
  11.3 2.9 %memory_sums.2 = (f32[8,136,128]{2,1,0:T(8,128)}, bf16[8,144,128]{2,1,0:T(8,128)(2,1)}) custom-call(s32[1]{0:T(128)S(6)} %copy.15.count.count_ref.refs_12_, bf16[256,2048]{1,0:T(8,128)(2,1)} %refs_1_.3, bf16[256,2048]{1,0:T(8,128)(2,1)} %refs_2_.3, f32[8,256]{1,0:T(8,128)} %get-tuple-element.70.rest_0_.run.rest_1_), custom_call_target="tpu_custom_call" | custom-call | tf_op jit(solution)/shard_map/memory_sums/pallas_call | solution.py:128
  14.2 0.5 collective-permute-start.8
  14.7 2.7 %gram_sums.2 = (f32[8,136,128]{2,1,0:T(8,128)}, bf16[8,144,128]{2,1,0:T(8,128)(2,1)}, bf16[8,128,256]{2,1,0:T(8,128)(2,1)}, f32[8,256]{1,0:T(8,128)}) custom-call(s32[1]{0:T(128)S(6)} %copy.15.count.count_ref.refs_12_, bf16[256,2048]{1,0:T(8,128)(2,1)} %refs_1_.3, f32[8,256]{1,0:T(8,128)} %get-tuple-element.70.rest_0_.run.rest_1_), custom_call_target="tpu_custom_call" | custom-call | tf_op jit(solution)/shard_map/gram_sums/pallas_call | solution.py:128
  17.5 0.7 copy-done.2
  18.2 2.0 %pair.7 = (f32[4,136,128]{2,1,0:T(8,128)}, bf16[4,144,128]{2,1,0:T(8,128)(2,1)}) custom-call(s32[1]{0:T(128)} %bitcast.side.refs_0_, f32[8,136,128]{2,1,0:T(8,128)} %get-tuple-element.63.own, bf16[8,144,128]{2,1,0:T(8,128)(2,1)} %copy-done.2), custom_call_target="tpu_custom_call" | custom-call | tf_op jit(solution)/shard_map/pair/pallas_call | solution.py:175
  20.2 3.0 %collective-permute-start.25 = (bf16[4,144,128]{2,1,0:T(8,128)(2,1)}, bf16[4,144,128]{2,1,0:T(8,128)(2,1)S(1)}, u32[]{:S(2)}, u32[]{:S(2)}) collective-permute-start(bf16[4,144,128]{2,1,0:T(8,128)(2,1)} %get-tuple-element.66), channel_id=1, source_target_pairs={{0,2},{1,3},{2,0},{3,1},{4,6},{5,7},{6,4},{7,5},{8,10},{9,11},{10,... | collective-permute-start | bytes 442376 | tf_op jit(solution)/shard_map/ppermute | solution.py:294
  23.2 1.5 collective-permute-start.26
  24.7 0.7 copy-done
  25.4 2.0 %pair.6 = (f32[4,136,128]{2,1,0:T(8,128)}, bf16[4,144,128]{2,1,0:T(8,128)(2,1)}) custom-call(s32[1]{0:T(128)} %bitcast.side.refs_0_, f32[8,136,128]{2,1,0:T(8,128)} %get-tuple-element.57.own, bf16[8,144,128]{2,1,0:T(8,128)(2,1)} %copy-done), custom_call_target="tpu_custom_call" | custom-call | tf_op jit(solution)/shard_map/pair/pallas_call | solution.py:175
  27.4 1.2 collective-permute-start.17
  28.7 1.5 collective-permute-start.18
  30.2 0.9 collective-permute-start.19
  31.0 2.0 %pair.5 = (f32[4,136,128]{2,1,0:T(8,128)}, bf16[4,144,128]{2,1,0:T(8,128)(2,1)}) custom-call(s32[1]{0:T(128)} %bitcast.side.refs_0_, f32[8,136,128]{2,1,0:T(8,128)} %get-tuple-element.47.own, bf16[8,144,128]{2,1,0:T(8,128)(2,1)} %copy-done.3), custom_call_target="tpu_custom_call" | custom-call | tf_op jit(solution)/shard_map/pair/pallas_call | solution.py:175
  33.0 1.9 %collective-permute-start.10 = (bf16[4,144,128]{2,1,0:T(8,128)(2,1)}, bf16[4,144,128]{2,1,0:T(8,128)(2,1)S(1)}, u32[]{:S(2)}, u32[]{:S(2)}) collective-permute-start(bf16[4,144,128]{2,1,0:T(8,128)(2,1)} %get-tuple-element.50), channel_id=1, source_target_pairs={{0,4},{1,5},{2,6},{3,7},{4,0},{5,1},{6,2},{7,3},{8,12},{9,13},{10,... | collective-permute-start | bytes 442376 | tf_op jit(solution)/shard_map/ppermute | solution.py:294
  35.0 0.6 collective-permute-start.11
  35.6 2.0 %pair.4 = (f32[4,136,128]{2,1,0:T(8,128)}, bf16[4,144,128]{2,1,0:T(8,128)(2,1)}) custom-call(s32[1]{0:T(128)} %bitcast.side.refs_0_, f32[8,136,128]{2,1,0:T(8,128)} %get-tuple-element.41.own, bf16[8,144,128]{2,1,0:T(8,128)(2,1)} %copy-done.1), custom_call_target="tpu_custom_call" | custom-call | tf_op jit(solution)/shard_map/pair/pallas_call | solution.py:175
  37.6 0.9 collective-permute-start.1
  38.6 3.2 %collective-permute-done.18.rest_1_ = bf16[4,144,128]{2,1,0:T(8,128)(2,1)S(1)} collective-permute-done((bf16[4,144,128]{2,1,0:T(8,128)(2,1)}, bf16[4,144,128]{2,1,0:T(8,128)(2,1)S(1)}, u32[]{:S(2)}, u32[]{:S(2)}) %collective-permute-start.18) | collective-permute-done | bytes 147488 | tf_op jit(solution)/shard_map/ppermute | solution.py:294
  41.8 2.4 %collective-permute-start.2 = (bf16[4,144,128]{2,1,0:T(8,128)(2,1)}, bf16[4,144,128]{2,1,0:T(8,128)(2,1)S(1)}, u32[]{:S(2)}, u32[]{:S(2)}) collective-permute-start(bf16[4,144,128]{2,1,0:T(8,128)(2,1)} %get-tuple-element.44), channel_id=1, source_target_pairs={{0,4},{1,5},{2,6},{3,7},{4,0},{5,1},{6,2},{7,3},{8,12},{9,13},{10,... | collective-permute-start | bytes 442376 | tf_op jit(solution)/shard_map/ppermute | solution.py:294
  44.2 2.2 %group.7 = (f32[4,136,128]{2,1,0:T(8,128)}, bf16[4,144,128]{2,1,0:T(8,128)(2,1)}, f32[4,136,128]{2,1,0:T(8,128)}) custom-call(s32[1]{0:T(128)} %bitcast.3.side, f32[4,136,128]{2,1,0:T(8,128)} %get-tuple-element.65.own, bf16[4,144,128]{2,1,0:T(8,128)(2,1)} %copy-done.25, bf16[4,144,128]{2,1,0:T(8,128)(2,1)} %copy-done.27, bf16[4,144,128]{2,1,0:T(8,128)(2,1)} %copy-done.29), custom_call_target="tpu_custom_call" | custom-call | tf_op jit(solution)/shard_map/group/pallas_call | solution.py:236
  46.7 1.2 collective-permute-start.9
  47.9 3.5 %collective-permute-start.28 = (bf16[4,144,128]{2,1,0:T(8,128)(2,1)}, bf16[4,144,128]{2,1,0:T(8,128)(2,1)S(1)}, u32[]{:S(2)}, u32[]{:S(2)}) collective-permute-start(bf16[4,144,128]{2,1,0:T(8,128)(2,1)} %get-tuple-element.67), channel_id=1, source_target_pairs={{0,8},{1,9},{2,10},{3,11},{4,12},{5,13},{6,14},{7,15},{8,16},{9,17... | collective-permute-start | bytes 442376 | tf_op jit(solution)/shard_map/ppermute | solution.py:294
  51.5 4.5 %collective-permute-start.29 = (bf16[4,144,128]{2,1,0:T(8,128)(2,1)}, bf16[4,144,128]{2,1,0:T(8,128)(2,1)S(1)}, u32[]{:S(2)}, u32[]{:S(2)}) collective-permute-start(bf16[4,144,128]{2,1,0:T(8,128)(2,1)} %get-tuple-element.67), channel_id=1, source_target_pairs={{0,16},{1,17},{2,18},{3,19},{4,20},{5,21},{6,22},{7,23},{8,24},{9,... | collective-permute-start | bytes 442376 | tf_op jit(solution)/shard_map/ppermute | solution.py:294
  56.0 2.2 %group.6 = (f32[4,136,128]{2,1,0:T(8,128)}, bf16[4,144,128]{2,1,0:T(8,128)(2,1)}, f32[4,136,128]{2,1,0:T(8,128)}) custom-call(s32[1]{0:T(128)} %bitcast.3.side, f32[4,136,128]{2,1,0:T(8,128)} %get-tuple-element.59.own, bf16[4,144,128]{2,1,0:T(8,128)(2,1)} %copy-done.24, bf16[4,144,128]{2,1,0:T(8,128)(2,1)} %copy-done.26, bf16[4,144,128]{2,1,0:T(8,128)(2,1)} %copy-done.28), custom_call_target="tpu_custom_call" | custom-call | tf_op jit(solution)/shard_map/group/pallas_call | solution.py:236
  58.2 1.3 collective-permute-start.20
  59.5 1.9 %collective-permute-start.21 = (bf16[4,144,128]{2,1,0:T(8,128)(2,1)}, bf16[4,144,128]{2,1,0:T(8,128)(2,1)S(1)}, u32[]{:S(2)}, u32[]{:S(2)}) collective-permute-start(bf16[4,144,128]{2,1,0:T(8,128)(2,1)} %get-tuple-element.61), channel_id=1, source_target_pairs={{0,16},{1,17},{2,18},{3,19},{4,20},{5,21},{6,22},{7,23},{8,24},{9,... | collective-permute-start | bytes 442376 | tf_op jit(solution)/shard_map/ppermute | solution.py:294
  61.4 2.1 %group.4 = (f32[4,136,128]{2,1,0:T(8,128)}, bf16[4,144,128]{2,1,0:T(8,128)(2,1)}, f32[4,136,128]{2,1,0:T(8,128)}) custom-call(s32[1]{0:T(128)} %bitcast.3.side, f32[4,136,128]{2,1,0:T(8,128)} %get-tuple-element.43.own, bf16[4,144,128]{2,1,0:T(8,128)(2,1)} %copy-done.30, bf16[4,144,128]{2,1,0:T(8,128)(2,1)} %copy-done.32, bf16[4,144,128]{2,1,0:T(8,128)(2,1)} %copy-done.33), custom_call_target="tpu_custom_call" | custom-call | tf_op jit(solution)/shard_map/group/pallas_call | solution.py:236
  63.6 1.3 collective-permute-start.22
  64.9 1.3 collective-permute-start.4
  66.2 1.3 collective-permute-start.5
  67.5 3.5 %collective-permute-start.6 = (bf16[4,144,128]{2,1,0:T(8,128)(2,1)}, bf16[4,144,128]{2,1,0:T(8,128)(2,1)S(1)}, u32[]{:S(2)}, u32[]{:S(2)}) collective-permute-start(bf16[4,144,128]{2,1,0:T(8,128)(2,1)} %get-tuple-element.45), channel_id=1, source_target_pairs={{0,24},{1,25},{2,26},{3,27},{4,28},{5,29},{6,30},{7,31}} | collective-permute-start | bytes 442376 | tf_op jit(solution)/shard_map/ppermute | solution.py:294
  71.1 17.5 %collective-permute-start.30 = (bf16[4,144,128]{2,1,0:T(8,128)(2,1)}, bf16[4,144,128]{2,1,0:T(8,128)(2,1)S(1)}, u32[]{:S(2)}, u32[]{:S(2)}) collective-permute-start(bf16[4,144,128]{2,1,0:T(8,128)(2,1)} %get-tuple-element.67), channel_id=1, source_target_pairs={{0,24},{1,25},{2,26},{3,27},{4,28},{5,29},{6,30},{7,31}} | collective-permute-start | bytes 442376 | tf_op jit(solution)/shard_map/ppermute | solution.py:294
  88.6 2.2 %group.5 = (f32[4,136,128]{2,1,0:T(8,128)}, bf16[4,144,128]{2,1,0:T(8,128)(2,1)}, f32[4,136,128]{2,1,0:T(8,128)}) custom-call(s32[1]{0:T(128)} %bitcast.3.side, f32[4,136,128]{2,1,0:T(8,128)} %get-tuple-element.49.own, bf16[4,144,128]{2,1,0:T(8,128)(2,1)} %copy-done.31, bf16[4,144,128]{2,1,0:T(8,128)(2,1)} %copy-done.22, bf16[4,144,128]{2,1,0:T(8,128)(2,1)} %copy-done.23), custom_call_target="tpu_custom_call" | custom-call | tf_op jit(solution)/shard_map/group/pallas_call | solution.py:236
  90.7 1.3 collective-permute-start.12
  92.1 2.5 %collective-permute-start.13 = (bf16[4,144,128]{2,1,0:T(8,128)(2,1)}, bf16[4,144,128]{2,1,0:T(8,128)(2,1)S(1)}, u32[]{:S(2)}, u32[]{:S(2)}) collective-permute-start(bf16[4,144,128]{2,1,0:T(8,128)(2,1)} %get-tuple-element.51), channel_id=1, source_target_pairs={{0,16},{1,17},{2,18},{3,19},{4,20},{5,21},{6,22},{7,23},{8,24},{9,... | collective-permute-start | bytes 442376 | tf_op jit(solution)/shard_map/ppermute | solution.py:294
  94.5 5.1 %collective-permute-start.14 = (bf16[4,144,128]{2,1,0:T(8,128)(2,1)}, bf16[4,144,128]{2,1,0:T(8,128)(2,1)S(1)}, u32[]{:S(2)}, u32[]{:S(2)}) collective-permute-start(bf16[4,144,128]{2,1,0:T(8,128)(2,1)} %get-tuple-element.51), channel_id=1, source_target_pairs={{0,24},{1,25},{2,26},{3,27},{4,28},{5,29},{6,30},{7,31}} | collective-permute-start | bytes 442376 | tf_op jit(solution)/shard_map/ppermute | solution.py:294
  99.6 0.6 pad_add_fusion.side
  100.2 2.1 %last.6.rest_0_ = f32[4,128,128]{2,1,0:T(8,128)} custom-call(s32[2]{0:T(128)} %pad_add_fusion.side, f32[16,128,128]{2,1,0:T(8,128)} %start.6, bf16[4,144,128]{2,1,0:T(8,128)(2,1)} %copy-done.12, bf16[4,144,128]{2,1,0:T(8,128)(2,1)} %copy-done.13, bf16[4,144,128]{2,1,0:T(8,128)(2,1)} %copy-done.15, f32[4,136,128]{2,1,0:T(8,128)} %get-tuple-element.62.rest_3_), custom_call_target="tpu_custom_call" | custom-call | tf_op jit(solution)/shard_map/last/pallas_call | solution.py:268
  102.4 0.6 copy-done.19
  103.0 2.1 %last.4.rest_0_ = f32[4,128,128]{2,1,0:T(8,128)} custom-call(s32[2]{0:T(128)} %pad_add_fusion.side, f32[16,128,128]{2,1,0:T(8,128)} %start.6, bf16[4,144,128]{2,1,0:T(8,128)(2,1)} %copy-done.14, bf16[4,144,128]{2,1,0:T(8,128)(2,1)} %copy-done.17, bf16[4,144,128]{2,1,0:T(8,128)(2,1)} %copy-done.19, f32[4,136,128]{2,1,0:T(8,128)} %get-tuple-element.46.rest_3_), custom_call_target="tpu_custom_call" | custom-call | tf_op jit(solution)/shard_map/last/pallas_call | solution.py:268
  105.2 0.6 copy-done.16
  105.8 2.1 %last.7.refs_8_ = f32[4,128,128]{2,1,0:T(8,128)} custom-call(s32[2]{0:T(128)} %pad_add_fusion.side, f32[16,128,128]{2,1,0:T(8,128)} %start.7, bf16[4,144,128]{2,1,0:T(8,128)(2,1)} %copy-done.10, bf16[4,144,128]{2,1,0:T(8,128)(2,1)} %copy-done.11, bf16[4,144,128]{2,1,0:T(8,128)(2,1)} %copy-done.16, f32[4,136,128]{2,1,0:T(8,128)} %get-tuple-element.68.rest_3_), custom_call_target="tpu_custom_call" | custom-call | tf_op jit(solution)/shard_map/last/pallas_call | solution.py:268
  108.0 0.6 copy-done.18
  108.7 2.2 %last.5.refs_8_ = f32[4,128,128]{2,1,0:T(8,128)} custom-call(s32[2]{0:T(128)} %pad_add_fusion.side, f32[16,128,128]{2,1,0:T(8,128)} %start.7, bf16[4,144,128]{2,1,0:T(8,128)(2,1)} %copy-done.18, bf16[4,144,128]{2,1,0:T(8,128)(2,1)} %copy-done.20, bf16[4,144,128]{2,1,0:T(8,128)(2,1)} %copy-done.21, f32[4,136,128]{2,1,0:T(8,128)} %get-tuple-element.52.rest_3_), custom_call_target="tpu_custom_call" | custom-call | tf_op jit(solution)/shard_map/last/pallas_call | solution.py:268
  111.3 0.6 squeeze.5.refs_5_
  111.9 0.6 reshape.30.refs_6_
  112.5 3.4 %weights.3 = (f32[8,256,256]{2,1,0:T(8,128)}, f32[8,128,256]{2,1,0:T(8,128)}) custom-call(s32[1]{0:T(128)S(6)} %copy.15.count.count_ref.refs_12_, bf16[256,2048]{1,0:T(8,128)(2,1)} %queries.3, f32[8,256]{1,0:T(8,128)} %get-tuple-element.69.rest_0_.run.rest_1_, f32[8,256]{1,0:T(8,128)} %get-tuple-element.54.norm), custom_call_target="tpu_custom_call" | custom-call | tf_op jit(solution)/shard_map/weights/pallas_call | solution.py:354
  115.9 3.4 %weights.2 = (f32[8,256,256]{2,1,0:T(8,128)}, f32[8,128,256]{2,1,0:T(8,128)}) custom-call(s32[1]{0:T(128)S(6)} %copy.15.count.count_ref.refs_12_, bf16[256,2048]{1,0:T(8,128)(2,1)} %queries.3, f32[8,256]{1,0:T(8,128)} %get-tuple-element.70.rest_0_.run.rest_1_, f32[8,256]{1,0:T(8,128)} %get-tuple-element.38.norm), custom_call_target="tpu_custom_call" | custom-call | tf_op jit(solution)/shard_map/weights/pallas_call | solution.py:354
  119.3 0.6 reshape.28.refs_6_
  119.9 0.6 squeeze.4.refs_5_
  120.5 1.4 copy.13.ridge
  121.9 0.7 copy-done.8
  122.6 22.7 %solve.3.refs_3_ = f32[8,128,256]{2,1,0:T(8,128)} custom-call(s32[1]{0:T(128)} %bitcast.side.refs_0_, bf16[256,2048]{1,0:T(8,128)(2,1)} %refs_1_.3, bf16[8,128,256]{2,1,0:T(8,128)(2,1)} %get-tuple-element.53.keyt, f32[8,128,256]{2,1,0:T(8,128)} %get-tuple-element.55.queries, f32[8,256,256]{2,1,0:T(8,128)} %get-tuple-element.56.weights.refs_4_, ...), custom_call_target="tpu_custom_call" | custom-call | tf_op jit(solution)/shard_map/solve/pallas_call | solution.py:480
  145.2 0.7 copy-done.9
  145.9 22.5 %solve.2.refs_3_ = f32[8,128,256]{2,1,0:T(8,128)} custom-call(s32[1]{0:T(128)} %bitcast.side.refs_0_, bf16[256,2048]{1,0:T(8,128)(2,1)} %refs_1_.3, bf16[8,128,256]{2,1,0:T(8,128)(2,1)} %get-tuple-element.37.keyt, f32[8,128,256]{2,1,0:T(8,128)} %get-tuple-element.39.queries, f32[8,256,256]{2,1,0:T(8,128)} %get-tuple-element.40.weights.refs_4_, ...), custom_call_target="tpu_custom_call" | custom-call | tf_op jit(solution)/shard_map/solve/pallas_call | solution.py:480
  168.4 0.7 copy-done.6
  169.1 8.4 %readout.2.refs_13_ = f32[256,2048]{1,0:T(8,128)} custom-call(s32[1]{0:T(128)} %bitcast.side.refs_0_, bf16[256,2048]{1,0:T(8,128)(2,1)} %refs_1_.3, bf16[256,2048]{1,0:T(8,128)(2,1)} %refs_2_.3, f32[8,128,256]{2,1,0:T(8,128)} %solve.3.refs_3_, f32[8,256,256]{2,1,0:T(8,128)} %get-tuple-element.56.weights.refs_4_, f32[8,1,256]{2,1,0:T(1,128)} %squeeze.5.refs_5_, ...), custom_call_target="tpu_custom_call" | custom-call | tf_op jit(solution)/shard_map/readout/pallas_call | solution.py:586
  177.5 0.7 copy-done.7
  178.2 8.7 %readout.3 = bf16[256,2048]{1,0:T(8,128)(2,1)} custom-call(s32[1]{0:T(128)} %bitcast.side.refs_0_, bf16[256,2048]{1,0:T(8,128)(2,1)} %refs_1_.3, bf16[256,2048]{1,0:T(8,128)(2,1)} %refs_2_.3, f32[8,128,256]{2,1,0:T(8,128)} %solve.2.refs_3_, f32[8,256,256]{2,1,0:T(8,128)} %get-tuple-element.40.weights.refs_4_, f32[8,1,256]{2,1,0:T(1,128)} %squeeze.4.refs_5_, ...), custom_call_target="tpu_custom_call" | custom-call | tf_op jit(solution)/shard_map/readout/pallas_call | solution.py:586
  (105 shorter events, 1.8 us)
Async XLA Ops:
  8.1 9.4 %collective-permute-start.24 = (bf16[8,144,128]{2,1,0:T(8,128)(2,1)}, bf16[8,144,128]{2,1,0:T(8,128)(2,1)S(1)}, u32[]{:S(2)}, u32[]{:S(2)}) collective-permute-start(bf16[8,144,128]{2,1,0:T(8,128)(2,1)} %get-tuple-element.64), channel_id=1, source_target_pairs={{0,1},{1,0},{2,3},{3,2},{4,5},{5,4},{6,7},{7,6},{8,9},{9,8},{10,11... | collective-permute-start | bytes 884744 | tf_op jit(solution)/shard_map/ppermute | solution.py:294
  11.3 13.4 %collective-permute-start.16 = (bf16[8,144,128]{2,1,0:T(8,128)(2,1)}, bf16[8,144,128]{2,1,0:T(8,128)(2,1)S(1)}, u32[]{:S(2)}, u32[]{:S(2)}) collective-permute-start(bf16[8,144,128]{2,1,0:T(8,128)(2,1)} %get-tuple-element.58), channel_id=1, source_target_pairs={{0,1},{1,0},{2,3},{3,2},{4,5},{5,4},{6,7},{7,6},{8,9},{9,8},{10,11... | collective-permute-start | bytes 884744 | tf_op jit(solution)/shard_map/ppermute | solution.py:294
  14.2 13.2 %collective-permute-start.8 = (bf16[8,144,128]{2,1,0:T(8,128)(2,1)}, bf16[8,144,128]{2,1,0:T(8,128)(2,1)S(1)}, u32[]{:S(2)}, u32[]{:S(2)}) collective-permute-start(bf16[8,144,128]{2,1,0:T(8,128)(2,1)} %get-tuple-element.48), channel_id=1, source_target_pairs={{0,1},{1,0},{2,3},{3,2},{4,5},{5,4},{6,7},{7,6},{8,9},{9,8},{10,11... | collective-permute-start | bytes 884744 | tf_op jit(solution)/shard_map/ppermute | solution.py:294
  17.5 11.2 %collective-permute-start = (bf16[8,144,128]{2,1,0:T(8,128)(2,1)}, bf16[8,144,128]{2,1,0:T(8,128)(2,1)S(1)}, u32[]{:S(2)}, u32[]{:S(2)}) collective-permute-start(bf16[8,144,128]{2,1,0:T(8,128)(2,1)} %get-tuple-element.42), channel_id=1, source_target_pairs={{0,1},{1,0},{2,3},{3,2},{4,5},{5,4},{6,7},{7,6},{8,9},{9,8},{10,11... | collective-permute-start | bytes 884744 | tf_op jit(solution)/shard_map/ppermute | solution.py:294
  17.5 0.7 copy-start.2
  20.2 10.0 %collective-permute-start.25 = (bf16[4,144,128]{2,1,0:T(8,128)(2,1)}, bf16[4,144,128]{2,1,0:T(8,128)(2,1)S(1)}, u32[]{:S(2)}, u32[]{:S(2)}) collective-permute-start(bf16[4,144,128]{2,1,0:T(8,128)(2,1)} %get-tuple-element.66), channel_id=1, source_target_pairs={{0,2},{1,3},{2,0},{3,1},{4,6},{5,7},{6,4},{7,5},{8,10},{9,11},{10,... | collective-permute-start | bytes 442376 | tf_op jit(solution)/shard_map/ppermute | solution.py:294
  23.2 9.9 %collective-permute-start.26 = (bf16[4,144,128]{2,1,0:T(8,128)(2,1)}, bf16[4,144,128]{2,1,0:T(8,128)(2,1)S(1)}, u32[]{:S(2)}, u32[]{:S(2)}) collective-permute-start(bf16[4,144,128]{2,1,0:T(8,128)(2,1)} %get-tuple-element.66), channel_id=1, source_target_pairs={{0,4},{1,5},{2,6},{3,7},{4,0},{5,1},{6,2},{7,3},{8,12},{9,13},{10,... | collective-permute-start | bytes 442376 | tf_op jit(solution)/shard_map/ppermute | solution.py:294
  24.7 0.8 copy-start
  24.7 10.3 %collective-permute-start.27 = (bf16[4,144,128]{2,1,0:T(8,128)(2,1)}, bf16[4,144,128]{2,1,0:T(8,128)(2,1)S(1)}, u32[]{:S(2)}, u32[]{:S(2)}) collective-permute-start(bf16[4,144,128]{2,1,0:T(8,128)(2,1)} %get-tuple-element.66), channel_id=1, source_target_pairs={{0,6},{1,7},{2,4},{3,5},{4,2},{5,3},{6,0},{7,1},{8,14},{9,15},{10,... | collective-permute-start | bytes 442376 | tf_op jit(solution)/shard_map/ppermute | solution.py:294
  27.4 3.6 %copy-start.3 = (bf16[8,144,128]{2,1,0:T(8,128)(2,1)}, bf16[8,144,128]{2,1,0:T(8,128)(2,1)S(1)}, u32[]{:S(2)}) copy-start(bf16[8,144,128]{2,1,0:T(8,128)(2,1)S(1)} %collective-permute-done.8.got.refs_10_) | copy-start | bytes 884740
  27.4 10.2 %collective-permute-start.17 = (bf16[4,144,128]{2,1,0:T(8,128)(2,1)}, bf16[4,144,128]{2,1,0:T(8,128)(2,1)S(1)}, u32[]{:S(2)}, u32[]{:S(2)}) collective-permute-start(bf16[4,144,128]{2,1,0:T(8,128)(2,1)} %get-tuple-element.60), channel_id=1, source_target_pairs={{0,2},{1,3},{2,0},{3,1},{4,6},{5,7},{6,4},{7,5},{8,10},{9,11},{10,... | collective-permute-start | bytes 442376 | tf_op jit(solution)/shard_map/ppermute | solution.py:294
  28.7 7.0 %copy-start.1 = (bf16[8,144,128]{2,1,0:T(8,128)(2,1)}, bf16[8,144,128]{2,1,0:T(8,128)(2,1)S(1)}, u32[]{:S(2)}) copy-start(bf16[8,144,128]{2,1,0:T(8,128)(2,1)S(1)} %collective-permute-done.got.rest_2_) | copy-start | bytes 884740
  28.7 13.1 %collective-permute-start.18 = (bf16[4,144,128]{2,1,0:T(8,128)(2,1)}, bf16[4,144,128]{2,1,0:T(8,128)(2,1)S(1)}, u32[]{:S(2)}, u32[]{:S(2)}) collective-permute-start(bf16[4,144,128]{2,1,0:T(8,128)(2,1)} %get-tuple-element.60), channel_id=1, source_target_pairs={{0,4},{1,5},{2,6},{3,7},{4,0},{5,1},{6,2},{7,3},{8,12},{9,13},{10,... | collective-permute-start | bytes 442376 | tf_op jit(solution)/shard_map/ppermute | solution.py:294
  30.2 14.0 %copy-start.25 = (bf16[4,144,128]{2,1,0:T(8,128)(2,1)}, bf16[4,144,128]{2,1,0:T(8,128)(2,1)S(1)}, u32[]{:S(2)}) copy-start(bf16[4,144,128]{2,1,0:T(8,128)(2,1)S(1)} %collective-permute-done.25.rest_0_) | copy-start | bytes 442372
  30.2 13.9 %collective-permute-start.19 = (bf16[4,144,128]{2,1,0:T(8,128)(2,1)}, bf16[4,144,128]{2,1,0:T(8,128)(2,1)S(1)}, u32[]{:S(2)}, u32[]{:S(2)}) collective-permute-start(bf16[4,144,128]{2,1,0:T(8,128)(2,1)} %get-tuple-element.60), channel_id=1, source_target_pairs={{0,6},{1,7},{2,4},{3,5},{4,2},{5,3},{6,0},{7,1},{8,14},{9,15},{10,... | collective-permute-start | bytes 442376 | tf_op jit(solution)/shard_map/ppermute | solution.py:294
  33.0 11.1 %copy-start.27 = (bf16[4,144,128]{2,1,0:T(8,128)(2,1)}, bf16[4,144,128]{2,1,0:T(8,128)(2,1)S(1)}, u32[]{:S(2)}) copy-start(bf16[4,144,128]{2,1,0:T(8,128)(2,1)S(1)} %collective-permute-done.26.rest_1_) | copy-start | bytes 442372
  33.0 13.7 %collective-permute-start.10 = (bf16[4,144,128]{2,1,0:T(8,128)(2,1)}, bf16[4,144,128]{2,1,0:T(8,128)(2,1)S(1)}, u32[]{:S(2)}, u32[]{:S(2)}) collective-permute-start(bf16[4,144,128]{2,1,0:T(8,128)(2,1)} %get-tuple-element.50), channel_id=1, source_target_pairs={{0,4},{1,5},{2,6},{3,7},{4,0},{5,1},{6,2},{7,3},{8,12},{9,13},{10,... | collective-permute-start | bytes 442376 | tf_op jit(solution)/shard_map/ppermute | solution.py:294
  35.0 9.2 %copy-start.29 = (bf16[4,144,128]{2,1,0:T(8,128)(2,1)}, bf16[4,144,128]{2,1,0:T(8,128)(2,1)S(1)}, u32[]{:S(2)}) copy-start(bf16[4,144,128]{2,1,0:T(8,128)(2,1)S(1)} %collective-permute-done.27.rest_2_) | copy-start | bytes 442372
  35.0 13.0 %collective-permute-start.11 = (bf16[4,144,128]{2,1,0:T(8,128)(2,1)}, bf16[4,144,128]{2,1,0:T(8,128)(2,1)S(1)}, u32[]{:S(2)}, u32[]{:S(2)}) collective-permute-start(bf16[4,144,128]{2,1,0:T(8,128)(2,1)} %get-tuple-element.50), channel_id=1, source_target_pairs={{0,6},{1,7},{2,4},{3,5},{4,2},{5,3},{6,0},{7,1},{8,14},{9,15},{10,... | collective-permute-start | bytes 442376 | tf_op jit(solution)/shard_map/ppermute | solution.py:294
  37.6 18.4 %copy-start.24 = (bf16[4,144,128]{2,1,0:T(8,128)(2,1)}, bf16[4,144,128]{2,1,0:T(8,128)(2,1)S(1)}, u32[]{:S(2)}) copy-start(bf16[4,144,128]{2,1,0:T(8,128)(2,1)S(1)} %collective-permute-done.17.rest_0_) | copy-start | bytes 442372
  37.6 13.8 %collective-permute-start.1 = (bf16[4,144,128]{2,1,0:T(8,128)(2,1)}, bf16[4,144,128]{2,1,0:T(8,128)(2,1)S(1)}, u32[]{:S(2)}, u32[]{:S(2)}) collective-permute-start(bf16[4,144,128]{2,1,0:T(8,128)(2,1)} %get-tuple-element.44), channel_id=1, source_target_pairs={{0,2},{1,3},{2,0},{3,1},{4,6},{5,7},{6,4},{7,5},{8,10},{9,11},{10,... | collective-permute-start | bytes 442376 | tf_op jit(solution)/shard_map/ppermute | solution.py:294
  41.7 14.2 %copy-start.26 = (bf16[4,144,128]{2,1,0:T(8,128)(2,1)}, bf16[4,144,128]{2,1,0:T(8,128)(2,1)S(1)}, u32[]{:S(2)}) copy-start(bf16[4,144,128]{2,1,0:T(8,128)(2,1)S(1)} %collective-permute-done.18.rest_1_) | copy-start | bytes 442372
  41.8 16.4 %collective-permute-start.2 = (bf16[4,144,128]{2,1,0:T(8,128)(2,1)}, bf16[4,144,128]{2,1,0:T(8,128)(2,1)S(1)}, u32[]{:S(2)}, u32[]{:S(2)}) collective-permute-start(bf16[4,144,128]{2,1,0:T(8,128)(2,1)} %get-tuple-element.44), channel_id=1, source_target_pairs={{0,4},{1,5},{2,6},{3,7},{4,0},{5,1},{6,2},{7,3},{8,12},{9,13},{10,... | collective-permute-start | bytes 442376 | tf_op jit(solution)/shard_map/ppermute | solution.py:294
  44.1 11.8 %copy-start.28 = (bf16[4,144,128]{2,1,0:T(8,128)(2,1)}, bf16[4,144,128]{2,1,0:T(8,128)(2,1)S(1)}, u32[]{:S(2)}) copy-start(bf16[4,144,128]{2,1,0:T(8,128)(2,1)S(1)} %collective-permute-done.19.rest_2_) | copy-start | bytes 442372
  44.1 15.3 %collective-permute-start.3 = (bf16[4,144,128]{2,1,0:T(8,128)(2,1)}, bf16[4,144,128]{2,1,0:T(8,128)(2,1)S(1)}, u32[]{:S(2)}, u32[]{:S(2)}) collective-permute-start(bf16[4,144,128]{2,1,0:T(8,128)(2,1)} %get-tuple-element.44), channel_id=1, source_target_pairs={{0,6},{1,7},{2,4},{3,5},{4,2},{5,3},{6,0},{7,1},{8,14},{9,15},{10,... | collective-permute-start | bytes 442376 | tf_op jit(solution)/shard_map/ppermute | solution.py:294
  46.7 41.8 %copy-start.22 = (bf16[4,144,128]{2,1,0:T(8,128)(2,1)}, bf16[4,144,128]{2,1,0:T(8,128)(2,1)S(1)}, u32[]{:S(2)}) copy-start(bf16[4,144,128]{2,1,0:T(8,128)(2,1)S(1)} %collective-permute-done.10.rest_1_) | copy-start | bytes 442372
  46.7 16.9 %collective-permute-start.9 = (bf16[4,144,128]{2,1,0:T(8,128)(2,1)}, bf16[4,144,128]{2,1,0:T(8,128)(2,1)S(1)}, u32[]{:S(2)}, u32[]{:S(2)}) collective-permute-start(bf16[4,144,128]{2,1,0:T(8,128)(2,1)} %get-tuple-element.50), channel_id=1, source_target_pairs={{0,2},{1,3},{2,0},{3,1},{4,6},{5,7},{6,4},{7,5},{8,10},{9,11},{10,... | collective-permute-start | bytes 442376 | tf_op jit(solution)/shard_map/ppermute | solution.py:294
  47.9 40.6 %copy-start.23 = (bf16[4,144,128]{2,1,0:T(8,128)(2,1)}, bf16[4,144,128]{2,1,0:T(8,128)(2,1)S(1)}, u32[]{:S(2)}) copy-start(bf16[4,144,128]{2,1,0:T(8,128)(2,1)S(1)} %collective-permute-done.11.rest_2_) | copy-start | bytes 442372
  47.9 16.9 %collective-permute-start.28 = (bf16[4,144,128]{2,1,0:T(8,128)(2,1)}, bf16[4,144,128]{2,1,0:T(8,128)(2,1)S(1)}, u32[]{:S(2)}, u32[]{:S(2)}) collective-permute-start(bf16[4,144,128]{2,1,0:T(8,128)(2,1)} %get-tuple-element.67), channel_id=1, source_target_pairs={{0,8},{1,9},{2,10},{3,11},{4,12},{5,13},{6,14},{7,15},{8,16},{9,17... | collective-permute-start | bytes 442376 | tf_op jit(solution)/shard_map/ppermute | solution.py:294
  51.4 10.0 %copy-start.30 = (bf16[4,144,128]{2,1,0:T(8,128)(2,1)}, bf16[4,144,128]{2,1,0:T(8,128)(2,1)S(1)}, u32[]{:S(2)}) copy-start(bf16[4,144,128]{2,1,0:T(8,128)(2,1)S(1)} %collective-permute-done.1.rest_0_) | copy-start | bytes 442372
  51.5 14.7 %collective-permute-start.29 = (bf16[4,144,128]{2,1,0:T(8,128)(2,1)}, bf16[4,144,128]{2,1,0:T(8,128)(2,1)S(1)}, u32[]{:S(2)}, u32[]{:S(2)}) collective-permute-start(bf16[4,144,128]{2,1,0:T(8,128)(2,1)} %get-tuple-element.67), channel_id=1, source_target_pairs={{0,16},{1,17},{2,18},{3,19},{4,20},{5,21},{6,22},{7,23},{8,24},{9,... | collective-permute-start | bytes 442376 | tf_op jit(solution)/shard_map/ppermute | solution.py:294
  58.2 3.3 %copy-start.32 = (bf16[4,144,128]{2,1,0:T(8,128)(2,1)}, bf16[4,144,128]{2,1,0:T(8,128)(2,1)S(1)}, u32[]{:S(2)}) copy-start(bf16[4,144,128]{2,1,0:T(8,128)(2,1)S(1)} %collective-permute-done.2.rest_1_) | copy-start | bytes 442372
  58.2 9.4 %collective-permute-start.20 = (bf16[4,144,128]{2,1,0:T(8,128)(2,1)}, bf16[4,144,128]{2,1,0:T(8,128)(2,1)S(1)}, u32[]{:S(2)}, u32[]{:S(2)}) collective-permute-start(bf16[4,144,128]{2,1,0:T(8,128)(2,1)} %get-tuple-element.61), channel_id=1, source_target_pairs={{0,8},{1,9},{2,10},{3,11},{4,12},{5,13},{6,14},{7,15},{8,16},{9,17... | collective-permute-start | bytes 442376 | tf_op jit(solution)/shard_map/ppermute | solution.py:294
  59.5 2.0 %copy-start.33 = (bf16[4,144,128]{2,1,0:T(8,128)(2,1)}, bf16[4,144,128]{2,1,0:T(8,128)(2,1)S(1)}, u32[]{:S(2)}) copy-start(bf16[4,144,128]{2,1,0:T(8,128)(2,1)S(1)} %collective-permute-done.3.rest_2_) | copy-start | bytes 442372
  59.5 11.6 %collective-permute-start.21 = (bf16[4,144,128]{2,1,0:T(8,128)(2,1)}, bf16[4,144,128]{2,1,0:T(8,128)(2,1)S(1)}, u32[]{:S(2)}, u32[]{:S(2)}) collective-permute-start(bf16[4,144,128]{2,1,0:T(8,128)(2,1)} %get-tuple-element.61), channel_id=1, source_target_pairs={{0,16},{1,17},{2,18},{3,19},{4,20},{5,21},{6,22},{7,23},{8,24},{9,... | collective-permute-start | bytes 442376 | tf_op jit(solution)/shard_map/ppermute | solution.py:294
  63.6 25.0 %copy-start.31 = (bf16[4,144,128]{2,1,0:T(8,128)(2,1)}, bf16[4,144,128]{2,1,0:T(8,128)(2,1)S(1)}, u32[]{:S(2)}) copy-start(bf16[4,144,128]{2,1,0:T(8,128)(2,1)S(1)} %collective-permute-done.9.rest_0_) | copy-start | bytes 442372
  63.6 27.2 %collective-permute-start.22 = (bf16[4,144,128]{2,1,0:T(8,128)(2,1)}, bf16[4,144,128]{2,1,0:T(8,128)(2,1)S(1)}, u32[]{:S(2)}, u32[]{:S(2)}) collective-permute-start(bf16[4,144,128]{2,1,0:T(8,128)(2,1)} %get-tuple-element.61), channel_id=1, source_target_pairs={{0,24},{1,25},{2,26},{3,27},{4,28},{5,29},{6,30},{7,31}} | collective-permute-start | bytes 442376 | tf_op jit(solution)/shard_map/ppermute | solution.py:294
  64.9 40.2 %copy-start.10 = (bf16[4,144,128]{2,1,0:T(8,128)(2,1)}, bf16[4,144,128]{2,1,0:T(8,128)(2,1)S(1)}, u32[]{:S(2)}) copy-start(bf16[4,144,128]{2,1,0:T(8,128)(2,1)S(1)} %collective-permute-done.28.rest_0_) | copy-start | bytes 442372
  64.9 27.1 %collective-permute-start.4 = (bf16[4,144,128]{2,1,0:T(8,128)(2,1)}, bf16[4,144,128]{2,1,0:T(8,128)(2,1)S(1)}, u32[]{:S(2)}, u32[]{:S(2)}) collective-permute-start(bf16[4,144,128]{2,1,0:T(8,128)(2,1)} %get-tuple-element.45), channel_id=1, source_target_pairs={{0,8},{1,9},{2,10},{3,11},{4,12},{5,13},{6,14},{7,15},{8,16},{9,17... | collective-permute-start | bytes 442376 | tf_op jit(solution)/shard_map/ppermute | solution.py:294
  66.2 38.9 %copy-start.11 = (bf16[4,144,128]{2,1,0:T(8,128)(2,1)}, bf16[4,144,128]{2,1,0:T(8,128)(2,1)S(1)}, u32[]{:S(2)}) copy-start(bf16[4,144,128]{2,1,0:T(8,128)(2,1)S(1)} %collective-permute-done.29.rest_1_) | copy-start | bytes 442372
  66.2 28.3 %collective-permute-start.5 = (bf16[4,144,128]{2,1,0:T(8,128)(2,1)}, bf16[4,144,128]{2,1,0:T(8,128)(2,1)S(1)}, u32[]{:S(2)}, u32[]{:S(2)}) collective-permute-start(bf16[4,144,128]{2,1,0:T(8,128)(2,1)} %get-tuple-element.45), channel_id=1, source_target_pairs={{0,16},{1,17},{2,18},{3,19},{4,20},{5,21},{6,22},{7,23},{8,24},{9,... | collective-permute-start | bytes 442376 | tf_op jit(solution)/shard_map/ppermute | solution.py:294
  67.5 32.7 %copy-start.12 = (bf16[4,144,128]{2,1,0:T(8,128)(2,1)}, bf16[4,144,128]{2,1,0:T(8,128)(2,1)S(1)}, u32[]{:S(2)}) copy-start(bf16[4,144,128]{2,1,0:T(8,128)(2,1)S(1)} %collective-permute-done.20.rest_0_) | copy-start | bytes 442372
  67.5 34.8 %collective-permute-start.6 = (bf16[4,144,128]{2,1,0:T(8,128)(2,1)}, bf16[4,144,128]{2,1,0:T(8,128)(2,1)S(1)}, u32[]{:S(2)}, u32[]{:S(2)}) collective-permute-start(bf16[4,144,128]{2,1,0:T(8,128)(2,1)} %get-tuple-element.45), channel_id=1, source_target_pairs={{0,24},{1,25},{2,26},{3,27},{4,28},{5,29},{6,30},{7,31}} | collective-permute-start | bytes 442376 | tf_op jit(solution)/shard_map/ppermute | solution.py:294
  71.1 29.2 %copy-start.13 = (bf16[4,144,128]{2,1,0:T(8,128)(2,1)}, bf16[4,144,128]{2,1,0:T(8,128)(2,1)S(1)}, u32[]{:S(2)}) copy-start(bf16[4,144,128]{2,1,0:T(8,128)(2,1)S(1)} %collective-permute-done.21.rest_1_) | copy-start | bytes 442372
  71.1 34.1 %collective-permute-start.30 = (bf16[4,144,128]{2,1,0:T(8,128)(2,1)}, bf16[4,144,128]{2,1,0:T(8,128)(2,1)S(1)}, u32[]{:S(2)}, u32[]{:S(2)}) collective-permute-start(bf16[4,144,128]{2,1,0:T(8,128)(2,1)} %get-tuple-element.67), channel_id=1, source_target_pairs={{0,24},{1,25},{2,26},{3,27},{4,28},{5,29},{6,30},{7,31}} | collective-permute-start | bytes 442376 | tf_op jit(solution)/shard_map/ppermute | solution.py:294
  90.7 9.5 %copy-start.15 = (bf16[4,144,128]{2,1,0:T(8,128)(2,1)}, bf16[4,144,128]{2,1,0:T(8,128)(2,1)S(1)}, u32[]{:S(2)}) copy-start(bf16[4,144,128]{2,1,0:T(8,128)(2,1)S(1)} %collective-permute-done.22.rest_2_) | copy-start | bytes 442372
  90.7 17.2 %collective-permute-start.12 = (bf16[4,144,128]{2,1,0:T(8,128)(2,1)}, bf16[4,144,128]{2,1,0:T(8,128)(2,1)S(1)}, u32[]{:S(2)}, u32[]{:S(2)}) collective-permute-start(bf16[4,144,128]{2,1,0:T(8,128)(2,1)} %get-tuple-element.51), channel_id=1, source_target_pairs={{0,8},{1,9},{2,10},{3,11},{4,12},{5,13},{6,14},{7,15},{8,16},{9,17... | collective-permute-start | bytes 442376 | tf_op jit(solution)/shard_map/ppermute | solution.py:294
  92.0 10.3 %copy-start.14 = (bf16[4,144,128]{2,1,0:T(8,128)(2,1)}, bf16[4,144,128]{2,1,0:T(8,128)(2,1)S(1)}, u32[]{:S(2)}) copy-start(bf16[4,144,128]{2,1,0:T(8,128)(2,1)S(1)} %collective-permute-done.4.rest_0_) | copy-start | bytes 442372
  92.1 15.9 %collective-permute-start.13 = (bf16[4,144,128]{2,1,0:T(8,128)(2,1)}, bf16[4,144,128]{2,1,0:T(8,128)(2,1)S(1)}, u32[]{:S(2)}, u32[]{:S(2)}) collective-permute-start(bf16[4,144,128]{2,1,0:T(8,128)(2,1)} %get-tuple-element.51), channel_id=1, source_target_pairs={{0,16},{1,17},{2,18},{3,19},{4,20},{5,21},{6,22},{7,23},{8,24},{9,... | collective-permute-start | bytes 442376 | tf_op jit(solution)/shard_map/ppermute | solution.py:294
  94.5 7.8 %copy-start.17 = (bf16[4,144,128]{2,1,0:T(8,128)(2,1)}, bf16[4,144,128]{2,1,0:T(8,128)(2,1)S(1)}, u32[]{:S(2)}) copy-start(bf16[4,144,128]{2,1,0:T(8,128)(2,1)S(1)} %collective-permute-done.5.rest_1_) | copy-start | bytes 442372
  94.5 13.4 %collective-permute-start.14 = (bf16[4,144,128]{2,1,0:T(8,128)(2,1)}, bf16[4,144,128]{2,1,0:T(8,128)(2,1)S(1)}, u32[]{:S(2)}, u32[]{:S(2)}) collective-permute-start(bf16[4,144,128]{2,1,0:T(8,128)(2,1)} %get-tuple-element.51), channel_id=1, source_target_pairs={{0,24},{1,25},{2,26},{3,27},{4,28},{5,29},{6,30},{7,31}} | collective-permute-start | bytes 442376 | tf_op jit(solution)/shard_map/ppermute | solution.py:294
  102.4 19.5 %collective-permute-start.23 = (f32[4,128,128]{2,1,0:T(8,128)}, f32[4,128,128]{2,1,0:T(8,128)S(1)}, u32[]{:S(2)}, u32[]{:S(2)}) collective-permute-start(f32[4,128,128]{2,1,0:T(8,128)} %last.6.rest_0_), channel_id=1, source_target_pairs={{0,1},{1,0},{2,3},{3,2},{4,5},{5,4},{6,7},{7,6},{8,9},{9,8},{10,11... | collective-permute-start | bytes 786440 | tf_op jit(solution)/shard_map/ppermute | solution.py:294
  105.1 6.2 %copy-start.5 = (f32[8,256]{1,0:T(8,128)S(1)}, f32[8,256]{1,0:T(8,128)}, u32[]{:S(2)}) copy-start(f32[8,256]{1,0:T(8,128)} %get-tuple-element.69.rest_0_.run.rest_1_) | copy-start | bytes 24580
  105.1 6.8 %copy-start.34 = (f32[8,256]{1,0:T(8,128)S(1)}, f32[8,256]{1,0:T(8,128)}, u32[]{:S(2)}) copy-start(f32[8,256]{1,0:T(8,128)} %get-tuple-element.54.norm) | copy-start | bytes 24580
  105.2 40.1 %collective-permute-start.7 = (f32[4,128,128]{2,1,0:T(8,128)}, f32[4,128,128]{2,1,0:T(8,128)S(1)}, u32[]{:S(2)}, u32[]{:S(2)}) collective-permute-start(f32[4,128,128]{2,1,0:T(8,128)} %last.4.rest_0_), channel_id=1, source_target_pairs={{0,1},{1,0},{2,3},{3,2},{4,5},{5,4},{6,7},{7,6},{8,9},{9,8},{10,11... | collective-permute-start | bytes 786440 | tf_op jit(solution)/shard_map/ppermute | solution.py:294
  107.9 60.5 %collective-permute-start.31 = (f32[4,128,128]{2,1,0:T(8,128)}, f32[4,128,128]{2,1,0:T(8,128)S(1)}, u32[]{:S(2)}, u32[]{:S(2)}) collective-permute-start(f32[4,128,128]{2,1,0:T(8,128)} %last.7.refs_8_), channel_id=1, source_target_pairs={{0,1},{1,0},{2,3},{3,2},{4,5},{5,4},{6,7},{7,6},{8,9},{9,8},{10,11... | collective-permute-start | bytes 786440 | tf_op jit(solution)/shard_map/ppermute | solution.py:294
  108.0 0.7 copy-start.21
  108.7 10.6 %copy-start.35 = (f32[8,256]{1,0:T(8,128)S(1)}, f32[8,256]{1,0:T(8,128)}, u32[]{:S(2)}) copy-start(f32[8,256]{1,0:T(8,128)} %get-tuple-element.38.norm) | copy-start | bytes 24580
  108.7 11.2 %copy-start.4 = (f32[8,256]{1,0:T(8,128)S(1)}, f32[8,256]{1,0:T(8,128)}, u32[]{:S(2)}) copy-start(f32[8,256]{1,0:T(8,128)} %get-tuple-element.70.rest_0_.run.rest_1_) | copy-start | bytes 24580
  108.7 11.8 %copy-start.36 = (f32[16,128]{1,0:T(8,128)S(1)}, f32[16,128]{1,0:T(8,128)}, u32[]{:S(2)}) copy-start(f32[16,128]{1,0:T(8,128)} %param.17) | copy-start | bytes 24580
  110.9 66.6 %collective-permute-start.15 = (f32[4,128,128]{2,1,0:T(8,128)}, f32[4,128,128]{2,1,0:T(8,128)S(1)}, u32[]{:S(2)}, u32[]{:S(2)}) collective-permute-start(f32[4,128,128]{2,1,0:T(8,128)} %last.5.refs_8_), channel_id=1, source_target_pairs={{0,1},{1,0},{2,3},{3,2},{4,5},{5,4},{6,7},{7,6},{8,9},{9,8},{10,11... | collective-permute-start | bytes 786440 | tf_op jit(solution)/shard_map/ppermute | solution.py:294
  145.2 0.7 copy-start.9
  168.4 0.7 copy-start.6
  177.5 0.7 copy-start.7
  (5 other events, 3.3 us)
